TPU v7x, 128 devices: a whole 4x4x4 slice. The times are simulated.
128 devices in a mesh: defocus: 8 (over x_lo, y), blk: 16 (over z, x_hi, core).
Axes of the slice: x: 4 (x_hi: 2, x_lo: 2; x = x_hi * 2 + x_lo), y: 4, z: 4, core: 2. Of those that a mesh axis runs over, the one named last changes fastest.
Arguments:
- images: bfloat16 [8, 16, 384, 384], P('defocus', 'blk'), may hold values from -6 to 6
- projections: bfloat16 [16, 384, 384], P('blk', 'defocus'), may hold values from -6 to 6
- ctf_row: int32 [8, 16], P('defocus', 'blk'), may hold values from 0 to 63
- defocus_term: float32 [64], replicated, may hold values from 100 to 400
- astig_term: float32 [64], replicated, may hold values from -40 to 40
- astig_cross: float32 [64], replicated, may hold values from -40 to 40
- phase_shift: float32 [64], replicated, may hold values from 0.1 to 1.5
Outputs:
- peak: float32 [8, 16, 384, 384], P('defocus', 'blk')
All inputs are finite; a program needn't handle non-finite values.
Results may differ from a plain program's by a relative error of at most 0.0095.
Values may be sent and summed in bfloat16 or wider, within the bound.
No kernel may reach another device: no remote copies, remote signals or barrier semaphores. Data moves between devices by JAX's collectives and lax.ppermute only.
A program may use at most 64 MiB of HBM per device.

v0:
```python
import math
import jax
import jax.numpy as jnp
from jax import lax
from jax.sharding import PartitionSpec as P


def section_tables(pixels):
    indices = jnp.arange(pixels, dtype=jnp.int32)
    phases = indices[:, None] * indices[None, :] % pixels
    angles = phases.astype(jnp.float32) * (2.0 * math.pi / pixels)
    cosine_table = jnp.cos(angles).astype(jnp.bfloat16)
    sine_table = jnp.sin(angles).astype(jnp.bfloat16)
    boundary_table = jnp.concatenate([cosine_table, -sine_table], axis=1)
    squared_lookup = jnp.concatenate(
        [
            jnp.concatenate([cosine_table, sine_table], axis=1),
            jnp.concatenate([-sine_table, cosine_table], axis=1),
        ],
        axis=0,
    )
    return (boundary_table, squared_lookup)


def transform(template_stack, boundary_table, squared_lookup):
    pixels = template_stack.shape[-1]
    halves = jnp.einsum(
        "xgs,so->xgo", template_stack, boundary_table, preferred_element_type=jnp.float32
    ).astype(jnp.bfloat16)
    stacked = jnp.concatenate([halves[:, :, :pixels], halves[:, :, pixels:]], axis=1)
    result = jnp.einsum("ua,tab->tub", squared_lookup, stacked, preferred_element_type=jnp.float32)
    return (result[:, :pixels], result[:, pixels:])


def ctf_gains(row_ids, defocus_term, astig_term, astig_cross, phase_shift, pixels):
    indices = jnp.arange(pixels, dtype=jnp.int32)
    signed = jnp.where(indices < pixels // 2, indices, indices - pixels)
    frequency = signed.astype(jnp.float32) / pixels
    row_freq = frequency[:, None]
    col_freq = frequency[None, :]
    radial = row_freq * row_freq + col_freq * col_freq
    stretch = row_freq * row_freq - col_freq * col_freq
    skewed = 2.0 * row_freq * col_freq
    matches = row_ids[:, None] == jnp.arange(defocus_term.shape[0], dtype=jnp.int32)[None, :]

    def select_row(lookup_table):
        return jnp.sum(jnp.where(matches, lookup_table[None, :], 0.0), axis=1)[:, None, None]

    chi_angle = (
        select_row(defocus_term) * radial
        + select_row(astig_term) * stretch
        + select_row(astig_cross) * skewed
        + select_row(phase_shift)
    )
    return -jnp.sin(chi_angle)


def correlate(
    spectrum_re, spectrum_im, factor, ctf_weight, plane_re, plane_im, boundary_table, squared_lookup
):
    pixels = spectrum_re.shape[-1]
    wide_re = plane_re.astype(jnp.float32)
    wide_im = plane_im.astype(jnp.float32)
    template_norm = jnp.sum((wide_re * wide_re + wide_im * wide_im)[None] * ctf_weight, axis=(1, 2))
    scaling = factor / jnp.sqrt(template_norm + 1e-06)[:, None, None]
    product_re = ((spectrum_re * wide_re + spectrum_im * wide_im) * scaling).astype(jnp.bfloat16)
    product_im = ((spectrum_im * wide_re - spectrum_re * wide_im) * scaling).astype(jnp.bfloat16)
    combined_parts = jnp.concatenate([product_re, product_im], axis=2)
    halves = jnp.einsum(
        "xgs,so->xgo", combined_parts, squared_lookup, preferred_element_type=jnp.float32
    ).astype(jnp.bfloat16)
    stacked = jnp.concatenate([halves[:, :, :pixels], halves[:, :, pixels:]], axis=1)
    return jnp.einsum("ua,tab->tub", boundary_table, stacked, preferred_element_type=jnp.float32)


def per_device(images, projections, ctf_row, defocus_term, astig_term, astig_cross, phase_shift):
    micrographs = images[0]
    pixels = micrographs.shape[-1]
    boundary_table, squared_lookup = section_tables(pixels)
    spectrum_re, spectrum_im = transform(micrographs, boundary_table, squared_lookup)
    power_local = jnp.sum(spectrum_re * spectrum_re + spectrum_im * spectrum_im, axis=0)
    power_total = lax.psum(power_local.astype(jnp.bfloat16), "blk").astype(jnp.float32)
    mean_power = power_total / (lax.axis_size("blk") * micrographs.shape[0])
    noise_power = mean_power + 0.05 * jnp.mean(mean_power)
    transfer_gain = ctf_gains(
        ctf_row[0], defocus_term, astig_term, astig_cross, phase_shift, pixels
    )
    factor = transfer_gain / noise_power[None]
    ctf_weight = transfer_gain * factor
    library = lax.all_gather(projections, "defocus", axis=1, tiled=True)
    initial = jnp.full(micrographs.shape, -jnp.inf, jnp.float32)
    arrived_re, arrived_im = transform(
        lax.all_gather(library, "blk", axis=0, tiled=True), boundary_table, squared_lookup
    )
    rounded = lax.optimization_barrier(
        (arrived_re.astype(jnp.bfloat16), arrived_im.astype(jnp.bfloat16))
    )

    def one_plane(current, planes):
        scores = correlate(
            spectrum_re,
            spectrum_im,
            factor,
            ctf_weight,
            planes[0],
            planes[1],
            boundary_table,
            squared_lookup,
        )
        return (jnp.maximum(current, scores), None)

    result, _ = lax.scan(one_plane, initial, (rounded[0], rounded[1]))
    return result[None]


def solution(mesh):
    in_specs = (
        P("defocus", "blk", None, None),
        P("blk", "defocus", None),
        P("defocus", "blk"),
        P(),
        P(),
        P(),
        P(),
    )
    out_specs = P("defocus", "blk", None, None)
    return jax.shard_map(
        per_device, mesh=mesh, in_specs=in_specs, out_specs=out_specs, check_vma=False
    )
```

profile of v0, /device:TPU:1, one launch (start us, length us, event | category | flops | bytes accessed | tf_op | source)
XLA Modules:
  0.0 378.4 jit_solution(12518729024491444624)
XLA Ops:
  15.7 25.8 %all_gather.6 = bf16[1,384,384]{2,1,0:T(8,128)(2,1)} all-gather(bf16[1,48,384]{2,1,0:T(8,128)(2,1)S(1)} %copy-done.2), channel_id=1, replica_groups=mesh['defocus'=8,'blk'=16] {'defocus'}, dimensions={1}, use_global_device_ids=true | all-gather | bytes 331776 | tf_op jit(solution)/shard_map/all_gather | solution.py:90
  46.1 104.6 %all-reduce.2.cloned.1.call-done = bf16[384,384]{0,1:T(8,128)(2,1)} async-done(((bf16[384,384]{0,1:T(8,128)(2,1)}), bf16[384,384]{0,1:T(8,128)(2,1)}) %all-reduce.2.cloned.1.call-update) | async-done | bytes 294928 | tf_op jit(solution)/shard_map/psum | solution.py:82
  153.0 6.9 %fusion.43 = (f32[1,384,384]{1,2,0:T(8,128)}, f32[1,384,384]{1,2,0:T(8,128)S(1)}) fusion(f32[]{:T(128)S(6)} %mul_shard_map.3, bf16[384,384]{0,1:T(8,128)(2,1)} %all-reduce.2.cloned.1.call-done, f32[]{:T(128)} %get-tuple-element.152, f32[384]{0:T(512)S(1)} %get-tuple-element.157, f32[384]{0:T(512)S(1)} %get-tuple-element.156, f32[]{:T(128)} %get-tuple-element.153, ...), kind=kLoop, calls=%fused_computation.76 | loop fusion | flops 2211840 | bytes 1479188 | tf_op jit(solution)/shard_map/div | solution.py:88
  161.5 49.6 %all-gather.2.cloned.1.call-done = bf16[16,384,384]{2,1,0:T(8,128)(2,1)} async-done(((bf16[1,384,384]{2,1,0:T(8,128)(2,1)}), bf16[16,384,384]{2,1,0:T(8,128)(2,1)}) %all-gather.2.cloned.1.call-update) | async-done | bytes 4718608 | tf_op jit(solution)/shard_map/all_gather | solution.py:93
  211.0 9.7 %convert_bitcast_fusion.1 = bf16[16,384,768]{2,1,0:T(8,128)(2,1)} fusion(bf16[16,384,384]{2,1,0:T(8,128)(2,1)} %all-gather.2.cloned.1.call-done, bf16[384,384]{1,0:T(8,128)(2,1)S(1)} %fusion.36, bf16[384,384]{1,0:T(8,128)(2,1)S(1)} %cosine_convert_fusion), kind=kOutput, calls=%fused_computation.35 | convolution fusion | flops 3629776896 | bytes 14745600 | tf_op jit(solution)/shard_map/xgs,so->xgo/dot_general | solution.py:27
  220.8 7.3 %fusion.46 = (bf16[16,384,384]{2,1,0:T(8,128)(2,1)S(1)}, bf16[16,384,384]{2,1,0:T(8,128)(2,1)}) fusion(bf16[16,384,768]{2,1,0:T(8,128)(2,1)} %convert_bitcast_fusion.1), kind=kLoop, calls=%fused_computation.79 | loop fusion | bytes 18874368 | tf_op jit(solution)/shard_map/slice | solution.py:30
  228.1 11.7 %convert_bitcast_fusion = bf16[16,768,384]{1,2,0:T(8,128)(2,1)} fusion(bf16[16,384,384]{2,1,0:T(8,128)(2,1)} %get-tuple-element.144, bf16[16,384,384]{2,1,0:T(8,128)(2,1)S(1)} %get-tuple-element.143, bf16[384,384]{1,0:T(8,128)(2,1)S(1)} %cosine_convert_fusion, bf16[384,384]{1,0:T(8,128)(2,1)S(1)} %fusion.36, bf16[384,384]{1,0:T(8,128)(2,1)S(1)} %sine_convert_fusion), kind=kOutput, calls=%fused_computation.34 | convolution fusion | flops 7276068864 | bytes 19759104 | tf_op jit(solution)/shard_map/ua,tab->tub/dot_general | solution.py:31
  239.8 8.9 %fusion.45 = (bf16[16,384,384]{1,2,0:T(8,128)(2,1)}, bf16[16,384,384]{1,2,0:T(8,128)(2,1)}) fusion(bf16[16,768,384]{1,2,0:T(8,128)(2,1)} %convert_bitcast_fusion), kind=kLoop, calls=%fused_computation.78 | loop fusion | bytes 18874368 | tf_op jit(solution)/shard_map/slice | solution.py:32
  248.7 120.8 %while.11 = (s32[]{:T(128)}, f32[1,384,384]{1,2,0:T(8,128)}, bf16[16,384,384]{1,2,0:T(8,128)(2,1)}, f32[1,384,384]{2,1,0:T(8,128)S(1)}, bf16[16,384,384]{1,2,0:T...) while((s32[]{:T(128)}, f32[1,384,384]{1,2,0:T(8,128)}, ...), condition=%wide.region_8.9_spmd.clone, body=%wide.region_6.8_spmd.clone.sunk | while | flops 685375488 | bytes 17105100 | solution.py:112
  261.0 2.6 fusion.64
  268.6 2.6 fusion.64
  276.2 2.6 fusion.64
  283.7 2.6 fusion.64
  291.3 2.6 fusion.64
  298.8 2.6 fusion.64
  306.4 2.6 fusion.64
  314.0 2.6 fusion.64
  321.5 2.6 fusion.64
  329.1 2.6 fusion.64
  336.6 2.6 fusion.64
  344.2 2.6 fusion.64
  351.8 2.6 fusion.64
  359.3 2.6 fusion.64
  366.9 2.6 fusion.64
  (181 shorter events, 88.6 us)
Async XLA Ops:
  6.5 7.0 %copy-start = (bf16[1,1,384,384]{3,2,1,0:T(8,128)(2,1)S(1)}, bf16[1,1,384,384]{3,2,1,0:T(8,128)(2,1)}, u32[]{:S(2)}) copy-start(bf16[1,1,384,384]{3,2,1,0:T(8,128)(2,1)} %param.9) | copy-start | bytes 884740
  6.5 144.1 %all-reduce.2.cloned.1.call-start = ((), (), s32[]{:S(2)}) async-start(), calls=%async_computation.1 | async-start | bytes 589824 | tf_op jit(solution)/shard_map/psum | solution.py:82
  14.7 1.0 copy-start.2
  14.8 27.9 %copy-start.3 = (f32[64]{0:T(128)S(1)}, f32[64]{0:T(128)}, u32[]{:S(2)}) copy-start(f32[64]{0:T(128)} %param.15) | copy-start | bytes 772
  14.8 27.9 %copy-start.4 = (f32[64]{0:T(128)S(1)}, f32[64]{0:T(128)}, u32[]{:S(2)}) copy-start(f32[64]{0:T(128)} %param.14) | copy-start | bytes 772
  14.8 28.6 %copy-start.5 = (f32[64]{0:T(128)S(1)}, f32[64]{0:T(128)}, u32[]{:S(2)}) copy-start(f32[64]{0:T(128)} %param.13) | copy-start | bytes 772
  14.8 28.6 %copy-start.6 = (f32[64]{0:T(128)S(1)}, f32[64]{0:T(128)}, u32[]{:S(2)}) copy-start(f32[64]{0:T(128)} %param.12) | copy-start | bytes 772
  15.7 195.4 %all-gather.2.cloned.1.call-start = ((), (), s32[]{:S(2)}) async-start(), calls=%async_computation | async-start | bytes 5013504 | tf_op jit(solution)/shard_map/all_gather | solution.py:93
  251.7 1.3 copy-start.1
  259.1 1.3 copy-start.1
  266.6 1.3 copy-start.1
  274.2 1.3 copy-start.1
  281.7 1.3 copy-start.1
  289.3 1.3 copy-start.1
  296.9 1.3 copy-start.1
  304.4 1.3 copy-start.1
  312.0 1.3 copy-start.1
  319.5 1.3 copy-start.1
  327.1 1.3 copy-start.1
  334.7 1.3 copy-start.1
  342.2 1.3 copy-start.1
  349.8 1.3 copy-start.1
  357.3 1.3 copy-start.1
  364.9 1.3 copy-start.1
Sparse Core Ops, SparseCore 0:
  15.8 134.7 all-reduce.1
  153.4 57.6 all-gather.1
where the time goes:
time: 380 us; the launch traced here: 378 us
  waiting for transfers between devices  154 us (41%)
  matrix products  73.6 us (19%)
  local copies, waits for them, and re-layouts  62.3 us (16%)
  other arithmetic  35.8 us (9%)
  blocking collectives  25.8 us (7%)
  between operations  14.9 us (4%)
  loops' own time  11.8 us (3%)
    psum x1, waiting for transfers between devices, per_device(): lax.psum(power_local.astype(jnp.bfloat16), 'blk').astype(jnp.float32)  105 us
    all_gather x1, waiting for transfers between devices, per_device(): lax.all_gather(library, 'blk', axis=0, tiled=True)  49.6 us
    dot_general x16, matrix products, correlate(): jnp.einsum('ua,tab->tub', boundary_table, stacked, preferred_element_type...  41 us
    all_gather x1, blocking collectives, per_device(): library = lax.all_gather(projections, 'defocus', axis=1, tiled=True)  25.8 us
    dynamic_slice x48, local copies, waits for them, and re-layouts, per_device(): result, _ = lax.scan(one_plane, initial, (rounded[0], rounded[1]))  24.7 us
    while x32, local copies, waits for them, and re-layouts  16.2 us
    dot_general x2, matrix products, transform(): jnp.einsum('ua,tab->tub', squared_lookup, stacked, preferred_element_type...  12.4 us
    reduce_sum x16, other arithmetic, correlate(): jnp.sum((wide_re * wide_re + wide_im * wide_im)[None] * ctf_weight, axis=...  12.1 us
  transfers between devices with their start and end apart: 2, of which 2 were waited for; matrix products, arithmetic and copies ran while one was open for 4% of the time, Pallas kernels for 0%

commit v1 on v0

--- a/solution.py
+++ b/solution.py
@@ -79,7 +79,9 @@
     boundary_table, squared_lookup = section_tables(pixels)
     spectrum_re, spectrum_im = transform(micrographs, boundary_table, squared_lookup)
     power_local = jnp.sum(spectrum_re * spectrum_re + spectrum_im * spectrum_im, axis=0)
-    power_total = lax.psum(power_local.astype(jnp.bfloat16), "blk").astype(jnp.float32)
+    power_total = jnp.sum(lax.all_gather(power_local.astype(jnp.bfloat16), "blk"), axis=0).astype(
+        jnp.float32
+    )
     mean_power = power_total / (lax.axis_size("blk") * micrographs.shape[0])
     noise_power = mean_power + 0.05 * jnp.mean(mean_power)
     transfer_gain = ctf_gains(

time: 380 us -> 297 us (0.78)
  waiting for transfers between devices: 154 us -> 72.8 us
    psum x1 -> x0, waiting for transfers between devices: 105 us -> none  [per_device(): lax.psum(power_local.astype(jnp.bfloat16), 'blk').astype(jnp.float32)]
    all_gather x0 -> x1, waiting for transfers between devices: none -> 20.2 us  [per_device(): lax.all_gather(power_local.astype(jnp.bfloat16), 'blk')]
  transfers between devices with their start and end apart: 2 -> 2, of which waited for: 2 -> 2; matrix products, arithmetic and copies ran while one was open for 4% -> 17% of each run, Pallas kernels for 0% -> 0%
where the time goes in v1:
time: 297 us; the launch traced here: 296 us
  matrix products  74.5 us (25%)
  waiting for transfers between devices  72.8 us (25%)
  local copies, waits for them, and re-layouts  62.5 us (21%)
  other arithmetic  34.6 us (12%)
  blocking collectives  25.8 us (9%)
  between operations  14.8 us (5%)
  loops' own time  10.6 us (4%)
    all_gather x1, waiting for transfers between devices, per_device(): lax.all_gather(library, 'blk', axis=0, tiled=True)  52.6 us
    dot_general x16, matrix products, correlate(): jnp.einsum('ua,tab->tub', boundary_table, stacked, preferred_element_type...  42 us
    all_gather x1, blocking collectives, per_device(): library = lax.all_gather(projections, 'defocus', axis=1, tiled=True)  25.8 us
    dynamic_slice x48, local copies, waits for them, and re-layouts, per_device(): result, _ = lax.scan(one_plane, initial, (rounded[0], rounded[1]))  24.7 us
    all_gather x1, waiting for transfers between devices, per_device(): lax.all_gather(power_local.astype(jnp.bfloat16), 'blk')  20.2 us
    while x32, local copies, waits for them, and re-layouts  16.2 us
    dot_general x2, matrix products, transform(): jnp.einsum('ua,tab->tub', squared_lookup, stacked, preferred_element_type...  12.4 us
    reduce_sum x16, other arithmetic, correlate(): jnp.sum((wide_re * wide_re + wide_im * wide_im)[None] * ctf_weight, axis=...  12 us
  transfers between devices with their start and end apart: 2, of which 2 were waited for; matrix products, arithmetic and copies ran while one was open for 17% of the time, Pallas kernels for 0%

profile of v1, /device:TPU:1, one launch (start us, length us, event | category | flops | bytes accessed | tf_op | source)
XLA Modules:
  0.0 295.8 jit_solution(8910089067790283671)
XLA Ops:
  6.5 25.8 %all_gather.10 = bf16[1,384,384]{2,1,0:T(8,128)(2,1)} all-gather(bf16[1,48,384]{2,1,0:T(8,128)(2,1)} %param.10), channel_id=1, replica_groups=mesh['defocus'=8,'blk'=16] {'defocus'}, dimensions={1}, use_global_device_ids=true | all-gather | bytes 331776 | tf_op jit(solution)/shard_map/all_gather | solution.py:92
  46.1 52.6 %all-gather.3.cloned.1.call-done = bf16[16,384,384]{2,1,0:T(8,128)(2,1)} async-done(((bf16[1,384,384]{2,1,0:T(8,128)(2,1)}), bf16[16,384,384]{2,1,0:T(8,128)(2,1)}) %all-gather.3.cloned.1.call-update) | async-done | bytes 4718608 | tf_op jit(solution)/shard_map/all_gather | solution.py:95
  98.7 9.7 %convert_bitcast_fusion.1 = bf16[16,384,768]{2,1,0:T(8,128)(2,1)} fusion(bf16[16,384,384]{2,1,0:T(8,128)(2,1)} %all-gather.3.cloned.1.call-done, bf16[384,384]{1,0:T(8,128)(2,1)S(1)} %fusion.36, bf16[384,384]{1,0:T(8,128)(2,1)S(1)} %cosine_convert_fusion), kind=kOutput, calls=%fused_computation.35 | convolution fusion | flops 3629776896 | bytes 14745600 | tf_op jit(solution)/shard_map/xgs,so->xgo/dot_general | solution.py:27
  108.4 7.4 %fusion.45 = (bf16[16,384,384]{2,1,0:T(8,128)(2,1)S(1)}, bf16[16,384,384]{2,1,0:T(8,128)(2,1)}) fusion(bf16[16,384,768]{2,1,0:T(8,128)(2,1)} %convert_bitcast_fusion.1), kind=kLoop, calls=%fused_computation.77 | loop fusion | bytes 18874368 | tf_op jit(solution)/shard_map/slice | solution.py:30
  115.8 11.7 %convert_bitcast_fusion = bf16[16,768,384]{1,2,0:T(8,128)(2,1)} fusion(bf16[16,384,384]{2,1,0:T(8,128)(2,1)} %get-tuple-element.144, bf16[16,384,384]{2,1,0:T(8,128)(2,1)S(1)} %get-tuple-element.143, bf16[384,384]{1,0:T(8,128)(2,1)S(1)} %cosine_convert_fusion, bf16[384,384]{1,0:T(8,128)(2,1)S(1)} %fusion.36, bf16[384,384]{1,0:T(8,128)(2,1)S(1)} %sine_convert_fusion), kind=kOutput, calls=%fused_computation.34 | convolution fusion | flops 7276068864 | bytes 19759104 | tf_op jit(solution)/shard_map/ua,tab->tub/dot_general | solution.py:31
  127.6 9.0 %fusion.44 = (bf16[16,384,384]{1,2,0:T(8,128)(2,1)}, bf16[16,384,384]{1,2,0:T(8,128)(2,1)}) fusion(bf16[16,768,384]{1,2,0:T(8,128)(2,1)} %convert_bitcast_fusion), kind=kLoop, calls=%fused_computation.76 | loop fusion | bytes 18874368 | tf_op jit(solution)/shard_map/slice | solution.py:32
  136.5 20.2 %all-gather.5.cloned.1.call-done = bf16[16,384,384]{2,1,0:T(8,128)(2,1)} async-done(((bf16[1,384,384]{2,1,0:T(8,128)(2,1)}), bf16[16,384,384]{2,1,0:T(8,128)(2,1)}) %all-gather.5.cloned.1.call-update) | async-done | bytes 4718608 | tf_op jit(solution)/shard_map/all_gather | solution.py:82
  156.7 3.1 %reduce_sum.74 = bf16[384,384]{1,0:T(8,128)(2,1)S(1)} reduce(bf16[16,384,384]{2,1,0:T(8,128)(2,1)} %all-gather.5.cloned.1.call-done, bf16[]{:T(256)} %constant.50.clone.1), dimensions={0}, to_apply=%region_4.5 | reduce | flops 2211840 | bytes 5013506 | tf_op jit(solution)/shard_map/reduce_sum | solution.py:82
  161.3 4.6 %bitcast_divide_fusion = (f32[1,384,384]{1,2,0:T(8,128)S(1)}, f32[1,384,384]{1,2,0:T(8,128)S(1)}) fusion(bf16[384,384]{0,1:T(8,128)(2,1)S(1)} %copy.27, f32[]{:T(128)S(6)} %mul_shard_map.3, f32[]{:T(128)} %get-tuple-element.152, f32[384]{0:T(512)S(1)} %get-tuple-element.157, f32[384]{0:T(512)S(1)} %get-tuple-element.156, f32[]{:T(128)} %get-tuple-element.153, ...), kind=kLoop, calls=%fused_computation.48 | loop fusion | flops 2211840 | bytes 1479188 | tf_op jit(solution)/shard_map/div | solution.py:90
  166.4 120.3 %while.11 = (s32[]{:T(128)}, f32[1,384,384]{1,2,0:T(8,128)}, bf16[16,384,384]{1,2,0:T(8,128)(2,1)}, f32[1,384,384]{2,1,0:T(8,128)S(1)}, bf16[16,384,384]{1,2,0:T...) while((s32[]{:T(128)}, f32[1,384,384]{1,2,0:T(8,128)}, ...), condition=%wide.region_8.9_spmd.clone, body=%wide.region_6.8_spmd.clone.sunk | while | flops 685375488 | bytes 17105100 | solution.py:114
  178.7 2.6 fusion.63
  186.2 2.6 fusion.63
  193.8 2.6 fusion.63
  201.3 2.6 fusion.63
  208.8 2.6 fusion.63
  216.4 2.6 fusion.63
  223.9 2.6 fusion.63
  231.4 2.6 fusion.63
  239.0 2.6 fusion.63
  246.5 2.6 fusion.63
  254.0 2.6 fusion.63
  261.6 2.6 fusion.63
  276.6 2.6 fusion.63
  284.2 2.6 fusion.63
  (182 shorter events, 89.4 us)
Async XLA Ops:
  6.5 32.8 %copy-start = (bf16[1,1,384,384]{3,2,1,0:T(8,128)(2,1)S(1)}, bf16[1,1,384,384]{3,2,1,0:T(8,128)(2,1)}, u32[]{:S(2)}) copy-start(bf16[1,1,384,384]{3,2,1,0:T(8,128)(2,1)} %param.9) | copy-start | bytes 884740
  6.5 92.2 %all-gather.3.cloned.1.call-start = ((), (), s32[]{:S(2)}) async-start(), calls=%async_computation | async-start | bytes 5013504 | tf_op jit(solution)/shard_map/all_gather | solution.py:95
  32.4 124.3 %all-gather.5.cloned.1.call-start = ((), (), s32[]{:S(2)}) async-start(), calls=%async_computation.1 | async-start | bytes 5013504 | tf_op jit(solution)/shard_map/all_gather | solution.py:82
  40.6 2.3 copy-start.2
  40.6 2.3 copy-start.3
  40.6 2.9 copy-start.4
  40.6 2.9 copy-start.5
  169.4 1.3 copy-start.1
  176.7 1.3 copy-start.1
  184.3 1.3 copy-start.1
  191.8 1.3 copy-start.1
  199.3 1.3 copy-start.1
  206.9 1.3 copy-start.1
  214.4 1.3 copy-start.1
  221.9 1.3 copy-start.1
  229.5 1.3 copy-start.1
  237.0 1.3 copy-start.1
  244.5 1.3 copy-start.1
  252.1 1.3 copy-start.1
  259.6 1.3 copy-start.1
  267.1 1.3 copy-start.1
  274.6 1.3 copy-start.1
  282.2 1.3 copy-start.1
Sparse Core Ops, SparseCore 0:
  32.5 66.2 all-gather.2
  101.2 55.4 all-gather.4
